TPU v7x, 256 devices: a whole 4x4x8 slice. The times are simulated.
256 devices in a mesh: member: 16 (over z_lo, x), grid: 16 (over z_hi, y, core).
Axes of the slice: x: 4, y: 4, z: 8 (z_hi: 2, z_lo: 4; z = z_hi * 4 + z_lo), core: 2. Of those that a mesh axis runs over, the one named last changes fastest.
Arguments:
- slabs: bfloat16 [16, 4096, 256], P('member', 'grid'), may hold values from -6 to 6
- loader: int32 [1], replicated, may hold values from 0 to 15
- hidden_jitter: bfloat16 [16, 2048, 16], P('member', 'grid'), may hold values from -3 to 3
- w_noise: bfloat16 [16, 1024], replicated, may hold values from -1.5 to 1.5
- w_enc: bfloat16 [128, 1024], replicated, may hold values from -0.10986328 to 0.10986328
- enc_offset: int32 [2048, 8], P('grid'), may hold values from -128 to 128
- enc_weight: float32 [2048, 8], P('grid'), may hold values from -1 to 1
- w_qkv: bfloat16 [1024, 1536], replicated, may hold values from -0.1875 to 0.1875
- window_offset: int32 [2048], P('grid'), may hold values from -64 to 0
- w_out: bfloat16 [512, 1024], replicated, may hold values from -0.25 to 0.25
- unpacker_linear_map: bfloat16 [1024, 128], replicated, may hold values from -0.1875 to 0.1875
- dec_offset: int32 [4096, 3], P('grid'), may hold values from -64 to 64
- unpacker_arc_scales: float32 [4096, 3], P('grid'), may hold values from 0.2 to 1
Outputs:
- grad_noise: float32 [16, 1024], P(None, ('member', 'grid'))
- grad_enc: float32 [128, 1024], P(None, ('member', 'grid'))
- grad_qkv: float32 [1024, 1536], P(('member', 'grid'))
- grad_out: float32 [512, 1024], P(None, ('member', 'grid'))
- unpacker_map_sensitivity: float32 [1024, 128], P(('member', 'grid'))
All inputs are finite; a program needn't handle non-finite values.
Results may differ from a plain program's by a relative error of at most 0.0075.
Values may be sent and summed in bfloat16 or wider, within the bound.
No kernel may reach another device: no remote copies, remote signals or barrier semaphores. Data moves between devices by JAX's collectives and lax.ppermute only.
A program may use at most 128 MiB of HBM per device.

v0:
```python
import jax
import jax.numpy as jnp
from jax import lax
from jax.sharding import PartitionSpec as P

HEAD_DIM = 64
RIM_G = 128
RIM_H = 64
WIN = 64
EPS = 1e-06
DELTA_SQ = 0.01


def extended(block, sides, width):
    for axis, dim in sides:
        count = lax.axis_size(axis)
        forward = [(i, i + 1) for i in range(count - 1)]
        forward.append((count - 1, 0))
        backward = [(target, source) for source, target in forward]
        low = lax.ppermute(
            lax.slice_in_dim(block, block.shape[dim] - width, None, axis=dim), axis, forward
        )
        high = lax.ppermute(lax.slice_in_dim(block, 0, width, axis=dim), axis, backward)
        block = jnp.concatenate([low, block, high], axis=dim)
    return block


def broadcast(x, axis, root):
    mine = lax.axis_index(axis) == root
    return lax.psum(jnp.where(mine, x, jnp.zeros_like(x)), axis)


def rms_factor(values):
    return lax.rsqrt(jnp.mean(values * values, axis=-1, keepdims=True) + EPS)


def rms_back(values, factor, gradient):
    inner = jnp.mean(gradient * values, axis=-1, keepdims=True)
    return factor * gradient - values * (factor * factor * factor) * inner


def silu_slope(pre):
    sigma = jax.nn.sigmoid(pre)
    return sigma * (1.0 + pre * (1.0 - sigma))


def eased_sensitivity(diff):
    return diff * lax.rsqrt(diff * diff + DELTA_SQ)


def plain_rims(values, depth):
    return extended(values, (("grid", 0),), depth)


def exact_rims(values, depth):
    return extended(values.astype(jnp.bfloat16), (("grid", 0),), depth).astype(values.dtype)


def fold_back(grad_ext, depth):
    edges = jnp.concatenate([grad_ext[:depth], grad_ext[-depth:]], axis=0)
    beside_all = exact_rims(edges, depth)
    inner_rows = grad_ext[depth:-depth]
    inner_rows = inner_rows.at[:depth].add(beside_all[:depth])
    return inner_rows.at[-depth:].add(beside_all[-depth:])


def realization_rotate(values):
    return lax.all_to_all(
        values.astype(jnp.bfloat16), "member", split_axis=0, concat_axis=0, tiled=True
    ).astype(values.dtype)


def rows_product(left, right):
    return lax.dot_general(
        left, right, (((0,), (0,)), ((), ())), preferred_element_type=jnp.float32
    )


def faithful_cells(left, right):
    return lax.dot_general(left, right, (((0,), (0,)), ((), ())), precision=lax.Precision.HIGHEST)


def cols_product(left, right):
    return lax.dot_general(
        left, right, (((1,), (1,)), ((), ())), preferred_element_type=jnp.float32
    )


def faithful_widths(left, right):
    return lax.dot_general(left, right, (((1,), (1,)), ((), ())), precision=lax.Precision.HIGHEST)


def per_device(
    slabs,
    loader,
    hidden_jitter,
    w_noise,
    w_enc,
    enc_offset,
    enc_weight,
    w_qkv,
    window_offset,
    w_out,
    unpacker_linear_map,
    dec_offset,
    unpacker_arc_scales,
):
    realization_array = lax.axis_size("member")
    shards = lax.axis_size("grid")
    analysis = broadcast(slabs[0], "member", loader[0])
    variable_tally = w_enc.shape[0]
    model_width = w_enc.shape[1]
    attn_width = w_out.shape[0]
    head_count = attn_width // HEAD_DIM
    lattice_cell_amounts = analysis.shape[0]
    node_rows = enc_offset.shape[0]
    inv_root = HEAD_DIM ** (-0.5)
    unadorned_state = analysis[:, :variable_tally]
    verifying_cell_amounts = analysis[:, variable_tally:]
    x_ext = plain_rims(unadorned_state, RIM_G)
    pre_enc = jnp.dot(x_ext, w_enc, preferred_element_type=jnp.float32)
    messages = jax.nn.silu(pre_enc).astype(jnp.bfloat16)
    home_rows = jnp.arange(node_rows, dtype=jnp.int32) * lattice_cell_amounts // node_rows
    enc_source = home_rows[:, None] + enc_offset + RIM_G
    averaged_cells = jnp.zeros((node_rows, model_width), jnp.float32)
    for arc_location in range(enc_offset.shape[1]):
        averaged_cells = averaged_cells + enc_weight[:, arc_location : arc_location + 1] * messages[
            enc_source[:, arc_location]
        ].astype(jnp.float32)
    factor0 = rms_factor(averaged_cells)
    jitter_cell_amounts = hidden_jitter[0]
    state0 = averaged_cells * factor0 + jnp.dot(
        jitter_cell_amounts, w_noise, preferred_element_type=jnp.float32
    )
    factor1 = rms_factor(state0)
    normed = (state0 * factor1).astype(jnp.bfloat16)
    mixed_rows = jnp.dot(normed, w_qkv, preferred_element_type=jnp.float32).reshape(
        node_rows, 3, head_count, HEAD_DIM
    )
    queries = mixed_rows[:, 0]
    key_raw = mixed_rows[:, 1]
    query_factor = rms_factor(queries)
    key_factor = rms_factor(key_raw)
    query_norm = (queries * query_factor).astype(jnp.bfloat16)
    key_norm = (key_raw * key_factor).astype(jnp.bfloat16)
    value_rows = mixed_rows[:, 2].astype(jnp.bfloat16)
    packed = jnp.concatenate(
        [key_norm.reshape(node_rows, attn_width), value_rows.reshape(node_rows, attn_width)], axis=1
    )
    packed_ext = plain_rims(packed, WIN)
    key_ext = packed_ext[:, :attn_width].reshape(-1, head_count, HEAD_DIM)
    value_ext = packed_ext[:, attn_width:].reshape(-1, head_count, HEAD_DIM)
    span_rows = node_rows + 2 * WIN
    relative = (
        jnp.arange(span_rows, dtype=jnp.int32)[None, :]
        - WIN
        - jnp.arange(node_rows, dtype=jnp.int32)[:, None]
    )
    starts = list(range(0, node_rows, node_rows))
    prob_blocks = []
    out_blocks = []
    for first_row in starts:
        query_block = query_norm
        key_block = key_ext
        value_block = value_ext
        offsets = window_offset[first_row : first_row + node_rows, None]
        allowed = ((relative >= offsets) & (relative < offsets + WIN)).astype(jnp.float32)
        scores = (
            jnp.einsum("qhd,khd->hqk", query_block, key_block, preferred_element_type=jnp.float32)
            * inv_root
        )
        weights_exp = jnp.exp(scores) * allowed[None]
        prob_block = (weights_exp / jnp.sum(weights_exp, axis=-1, keepdims=True)).astype(
            jnp.bfloat16
        )
        prob_blocks.append(prob_block)
        out_blocks.append(
            jnp.einsum(
                "hqk,khd->qhd", prob_block, value_block, preferred_element_type=jnp.float32
            ).astype(jnp.bfloat16)
        )
    attended = out_blocks[0].reshape(node_rows, attn_width)
    state1 = state0 + jnp.dot(attended, w_out, preferred_element_type=jnp.float32)
    factor2 = rms_factor(state1)
    dnorm = (state1 * factor2).astype(jnp.bfloat16)
    home_nodes = (
        jnp.arange(lattice_cell_amounts, dtype=jnp.int32) * node_rows // lattice_cell_amounts
    )
    unpacker_start_cell = home_nodes[:, None] + dec_offset + RIM_H
    dnorm_ext = plain_rims(dnorm, RIM_H)
    assembled_cells = jnp.zeros((lattice_cell_amounts, model_width), jnp.float32)
    for arc_location in range(dec_offset.shape[1]):
        assembled_cells = assembled_cells + unpacker_arc_scales[
            :, arc_location : arc_location + 1
        ] * dnorm_ext[unpacker_start_cell[:, arc_location]].astype(jnp.float32)
    restored_cells = jnp.dot(
        assembled_cells, unpacker_linear_map.astype(jnp.float32), precision=lax.Precision.HIGHEST
    )
    prognosis_cells = unadorned_state.astype(jnp.float32) + restored_cells
    subset_cells = lattice_cell_amounts // realization_array
    realization_cells = realization_rotate(
        prognosis_cells.reshape(realization_array, subset_cells, variable_tally)
    )
    member_index = lax.axis_index("member")
    truth_block = lax.dynamic_slice_in_dim(
        verifying_cell_amounts, member_index * subset_cells, subset_cells, 0
    ).astype(jnp.float32)
    loss_scale = float(realization_array * lattice_cell_amounts * shards * variable_tally) ** (-0.5)
    verifying_sensitivity = eased_sensitivity(realization_cells - truth_block[None])
    duo_spread_sum = jnp.sum(
        eased_sensitivity(realization_cells[:, None] - realization_cells[None, :]), axis=1
    )
    realization_sensitivity_array = (
        verifying_sensitivity / realization_array
        - duo_spread_sum / (realization_array * (realization_array - 1))
    ) * loss_scale
    prognosis_sensitivity = realization_rotate(realization_sensitivity_array).reshape(
        lattice_cell_amounts, variable_tally
    )
    assembled_sensitivity = faithful_widths(
        prognosis_sensitivity, unpacker_linear_map.astype(jnp.float32)
    )
    unpacker_map_sensitivity = faithful_cells(assembled_cells, prognosis_sensitivity)
    grad_dnorm_ext = jnp.zeros(dnorm_ext.shape, jnp.float32)
    for arc_location in range(dec_offset.shape[1]):
        grad_dnorm_ext = grad_dnorm_ext.at[unpacker_start_cell[:, arc_location]].add(
            unpacker_arc_scales[:, arc_location : arc_location + 1] * assembled_sensitivity
        )
    grad_dnorm = fold_back(grad_dnorm_ext, RIM_H)
    grad_state1 = rms_back(state1, factor2, grad_dnorm)
    grad_state1_b = grad_state1.astype(jnp.bfloat16)
    grad_out = rows_product(attended, grad_state1_b)
    grad_attended = (
        cols_product(grad_state1_b, w_out)
        .astype(jnp.bfloat16)
        .reshape(node_rows, head_count, HEAD_DIM)
    )
    grad_packed_ext = jnp.zeros((node_rows + 2 * WIN, 2 * attn_width), jnp.float32)
    grad_query_blocks = []
    for block_index, first_row in enumerate(starts):
        query_block = query_norm
        key_block = key_ext
        value_block = value_ext
        prob_block = prob_blocks[block_index]
        grad_probs = jnp.einsum(
            "qhd,khd->hqk", grad_attended, value_block, preferred_element_type=jnp.float32
        )
        prob_wide = prob_block.astype(jnp.float32)
        grad_scores = (
            prob_wide * (grad_probs - jnp.sum(prob_wide * grad_probs, axis=-1, keepdims=True))
        ).astype(jnp.bfloat16)
        grad_query_blocks.append(
            jnp.einsum("hqk,khd->qhd", grad_scores, key_block, preferred_element_type=jnp.float32)
            * inv_root
        )
        grad_key_block = (
            jnp.einsum("hqk,qhd->khd", grad_scores, query_block, preferred_element_type=jnp.float32)
            * inv_root
        )
        grad_value_block = jnp.einsum(
            "hqk,qhd->khd", prob_block, grad_attended, preferred_element_type=jnp.float32
        )
        grad_pair = jnp.concatenate(
            [
                grad_key_block.reshape(span_rows, attn_width),
                grad_value_block.reshape(span_rows, attn_width),
            ],
            axis=1,
        )
        grad_packed_ext = grad_packed_ext.at[first_row : first_row + span_rows].add(grad_pair)
    grad_packed = fold_back(grad_packed_ext, WIN)
    grad_knorm = grad_packed[:, :attn_width].reshape(node_rows, head_count, HEAD_DIM)
    grad_values = grad_packed[:, attn_width:].reshape(node_rows, head_count, HEAD_DIM)
    grad_qnorm = grad_query_blocks[0]
    grad_queries = rms_back(queries, query_factor, grad_qnorm)
    grad_keys = rms_back(key_raw, key_factor, grad_knorm)
    grad_mixed = (
        jnp.stack([grad_queries, grad_keys, grad_values], axis=1)
        .reshape(node_rows, 3 * attn_width)
        .astype(jnp.bfloat16)
    )
    grad_qkv = rows_product(normed, grad_mixed)
    grad_normed = cols_product(grad_mixed, w_qkv)
    grad_state0 = grad_state1 + rms_back(state0, factor1, grad_normed)
    grad_noise = rows_product(jitter_cell_amounts, grad_state0.astype(jnp.bfloat16))
    grad_pooled = rms_back(averaged_cells, factor0, grad_state0)
    grad_messages = jnp.zeros((x_ext.shape[0], model_width), jnp.float32)
    for arc_location in range(enc_offset.shape[1]):
        grad_messages = grad_messages.at[enc_source[:, arc_location]].add(
            enc_weight[:, arc_location : arc_location + 1] * grad_pooled
        )
    grad_enc = faithful_cells(x_ext.astype(jnp.float32), grad_messages * silu_slope(pre_enc))
    grad_noise, grad_enc, grad_qkv, grad_out, unpacker_map_sensitivity = (
        lax.psum_scatter(grad_noise, ("member", "grid"), scatter_dimension=1, tiled=True),
        lax.psum_scatter(grad_enc, ("member", "grid"), scatter_dimension=1, tiled=True),
        lax.psum_scatter(grad_qkv, ("member", "grid"), scatter_dimension=0, tiled=True),
        lax.psum_scatter(grad_out, ("member", "grid"), scatter_dimension=1, tiled=True),
        lax.psum_scatter(
            unpacker_map_sensitivity, ("member", "grid"), scatter_dimension=0, tiled=True
        ),
    )
    return (grad_noise, grad_enc, grad_qkv, grad_out, unpacker_map_sensitivity)


def solution(mesh):
    in_specs = (
        P("member", "grid", None),
        P(),
        P("member", "grid", None),
        P(),
        P(),
        P("grid", None),
        P("grid", None),
        P(),
        P("grid"),
        P(),
        P(),
        P("grid", None),
        P("grid", None),
    )
    out_specs = (
        P(None, ("member", "grid")),
        P(None, ("member", "grid")),
        P(("member", "grid"), None),
        P(None, ("member", "grid")),
        P(("member", "grid"), None),
    )
    return jax.shard_map(
        per_device, mesh=mesh, in_specs=in_specs, out_specs=out_specs, check_vma=False
    )
```

profile of v0, /device:TPU:8, one launch (start us, length us, event | category | flops | bytes accessed | tf_op | source)
XLA Modules:
  0.0 715.8 jit_solution(16894193995473229864)
XLA Ops:
  16.0 158.6 %all-reduce.9.cloned.1.call-done = bf16[256,256]{1,0:T(8,128)(2,1)} async-done(((bf16[256,256]{1,0:T(8,128)(2,1)}), bf16[256,256]{1,0:T(8,128)(2,1)}) %all-reduce.9.cloned.1.call-update) | async-done | bytes 131088 | tf_op jit(solution)/shard_map/psum | solution.py:30
  214.9 3.8 collective-permute-done.2
  232.4 3.6 gather_fusion.8
  245.9 6.5 all-to-all-start
  253.2 7.8 %all-to-all-done = bf16[16,16,128]{2,1,0:T(8,128)(2,1)} async-done(((bf16[16,16,128]{2,1,0:T(8,128)(2,1)}), bf16[16,16,128]{2,1,0:T(8,128)(2,1)}, u32[]{:S(2)}, u32[]{:S(2)}) %all-to-all-start) | async-done | bytes 65568 | tf_op jit(solution)/shard_map/all_to_all | solution.py:68
  263.7 4.1 all-to-all-start.1
  270.2 6.1 all-to-all-done.1
  278.5 4.6 scatter_custom_fusion
  283.2 5.6 scatter_custom_fusion.1
  288.8 5.6 scatter_custom_fusion.2
  295.8 5.6 collective-permute-start.6
  317.0 6.5 collective-permute-start.8
  323.5 6.2 collective-permute-start.9
  349.1 3.7 fusion.87
  356.1 3.7 scatter_custom_fusion.3
  359.8 5.1 scatter_custom_fusion.4
  364.9 5.1 scatter_custom_fusion.5
  370.1 5.1 scatter_custom_fusion.6
  375.2 5.1 scatter_custom_fusion.7
  380.3 5.1 scatter_custom_fusion.8
  385.4 5.3 scatter_custom_fusion.9
  390.8 5.1 scatter_custom_fusion.10
  395.9 5.2 fusion.3
  401.1 301.0 %all-reduce.11.cloned.1.call-done = (f32[16,1024]{1,0:T(8,128)}, f32[128,1024]{0,1:T(8,128)}, f32[1024,1536]{1,0:T(8,128)}, f32[512,1024]{0,1:T(8,128)}, f32[1024,128]{1,0:T(8,128)}) async-done(((f32[16,1024]{1,0:T(8,128)}, f32[128,1024]{0,1:T(8,128)}, f32[1024,1536]{1,0:T(8,128)}, f32[512,1024]{0,1:T(8,128)}, f32[1024,128]{1,0:T(8,128)}), (f32[16,1024]{1,0:T(8,128)}, f32[128,1024]{0,1:T(8,128)}, ...) | async-done | bytes 9502736
  (271 shorter events, 125.7 us)
Async XLA Ops:
  7.2 202.7 %copy-start = (bf16[1024,1536]{1,0:T(8,128)(2,1)S(1)}, bf16[1024,1536]{1,0:T(8,128)(2,1)}, u32[]{:S(2)}) copy-start(bf16[1024,1536]{1,0:T(8,128)(2,1)} %param.32) | copy-start | bytes 9437188
  7.2 167.5 %all-reduce.9.cloned.1.call-start = ((), (), s32[]{:S(2)}) async-start(), calls=%async_computation.2 | async-start | bytes 262144 | tf_op jit(solution)/shard_map/psum | solution.py:30
  9.5 172.6 %copy-start.58 = (s32[128]{0:T(128)}, s32[128]{0:T(128)S(1)}, u32[]{:S(2)}) copy-start(s32[128]{0:T(128)S(1)} %get-tuple-element.141) | copy-start | bytes 1540
  10.5 195.7 %copy-start.31 = (f32[128]{0:T(128)}, f32[128]{0:T(128)S(1)}, u32[]{:S(2)}) copy-start(f32[128]{0:T(128)S(1)} %get-tuple-element.132) | copy-start | bytes 1540
  10.5 195.7 %copy-start.33 = (f32[128]{0:T(128)}, f32[128]{0:T(128)S(1)}, u32[]{:S(2)}) copy-start(f32[128]{0:T(128)S(1)} %get-tuple-element.138) | copy-start | bytes 1540
  10.6 195.7 %copy-start.35 = (f32[128]{0:T(128)}, f32[128]{0:T(128)S(1)}, u32[]{:S(2)}) copy-start(f32[128]{0:T(128)S(1)} %get-tuple-element.139) | copy-start | bytes 1540
  10.6 195.7 %copy-start.37 = (f32[128]{0:T(128)}, f32[128]{0:T(128)S(1)}, u32[]{:S(2)}) copy-start(f32[128]{0:T(128)S(1)} %get-tuple-element.133) | copy-start | bytes 1540
  10.6 195.7 %copy-start.39 = (f32[128]{0:T(128)}, f32[128]{0:T(128)S(1)}, u32[]{:S(2)}) copy-start(f32[128]{0:T(128)S(1)} %get-tuple-element.134) | copy-start | bytes 1540
  10.6 195.7 %copy-start.41 = (f32[128]{0:T(128)}, f32[128]{0:T(128)S(1)}, u32[]{:S(2)}) copy-start(f32[128]{0:T(128)S(1)} %get-tuple-element.135) | copy-start | bytes 1540
  10.6 195.7 %copy-start.43 = (f32[128]{0:T(128)}, f32[128]{0:T(128)S(1)}, u32[]{:S(2)}) copy-start(f32[128]{0:T(128)S(1)} %get-tuple-element.136) | copy-start | bytes 1540
  10.6 195.7 %copy-start.45 = (f32[128]{0:T(128)}, f32[128]{0:T(128)S(1)}, u32[]{:S(2)}) copy-start(f32[128]{0:T(128)S(1)} %get-tuple-element.137) | copy-start | bytes 1540
  175.4 3.3 collective-permute-start
  175.4 3.3 collective-permute-start.1
  212.8 5.9 collective-permute-start.2
  214.5 4.3 collective-permute-start.3
  226.7 4.9 collective-permute-start.4
  228.5 3.1 collective-permute-start.5
  245.9 15.0 %all-to-all-start = ((bf16[16,16,128]{2,1,0:T(8,128)(2,1)}), bf16[16,16,128]{2,1,0:T(8,128)(2,1)}, u32[]{:S(2)}, u32[]{:S(2)}) async-start(bf16[16,16,128]{2,1,0:T(8,128)(2,1)} %bitcast.159), calls=%async_computation | async-start | bytes 131072 | tf_op jit(solution)/shard_map/all_to_all | solution.py:68
  263.7 12.6 %all-to-all-start.1 = ((bf16[16,16,128]{2,1,0:T(8,128)(2,1)}), bf16[16,16,128]{2,1,0:T(8,128)(2,1)}, u32[]{:S(2)}, u32[]{:S(2)}) async-start(bf16[16,16,128]{2,1,0:T(8,128)(2,1)} %multiply_convert_fusion.4), calls=%async_computation.1 | async-start | bytes 131072 | tf_op jit(solution)/shard_map/all_to_all | solution.py:68
  267.9 434.2 %all-reduce.11.cloned.1.call-start = ((), (), s32[]{:S(2)}) async-start(), calls=%async_computation.3 | async-start | bytes 19005440
  295.8 9.6 %collective-permute-start.6 = (bf16[64,1024]{1,0:T(8,128)(2,1)S(1)}, bf16[64,1024]{1,0:T(8,128)(2,1)S(1)}, u32[]{:S(2)}, u32[]{:S(2)}) collective-permute-start(bf16[64,1024]{1,0:T(8,128)(2,1)S(1)} %get-tuple-element.109), channel_id=1, source_target_pairs={{0,1},{1,2},{2,3},{3,4},{4,5},{5,6},{6,7},{7,8},{8,9},{9,10},{10,1... | collective-permute-start | bytes 393224 | tf_op jit(solution)/shard_map/ppermute | solution.py:20
  301.4 4.0 collective-permute-start.7
  317.0 16.2 %collective-permute-start.8 = (bf16[64,1024]{0,1:T(8,128)(2,1)S(1)}, bf16[64,1024]{0,1:T(8,128)(2,1)S(1)}, u32[]{:S(2)}, u32[]{:S(2)}) collective-permute-start(bf16[64,1024]{0,1:T(8,128)(2,1)S(1)} %get-tuple-element.107), channel_id=1, source_target_pairs={{0,1},{1,2},{2,3},{3,4},{4,5},{5,6},{6,7},{7,8},{8,9},{9,10},{10,1... | collective-permute-start | bytes 393224 | tf_op jit(solution)/shard_map/ppermute | solution.py:20
  323.5 10.1 %collective-permute-start.9 = (bf16[64,1024]{0,1:T(8,128)(2,1)S(1)}, bf16[64,1024]{0,1:T(8,128)(2,1)S(1)}, u32[]{:S(2)}, u32[]{:S(2)}) collective-permute-start(bf16[64,1024]{0,1:T(8,128)(2,1)S(1)} %get-tuple-element.108), channel_id=1, source_target_pairs={{1,0},{2,1},{3,2},{4,3},{5,4},{6,5},{7,6},{8,7},{9,8},{10,9},{11,1... | collective-permute-start | bytes 393224 | tf_op jit(solution)/shard_map/ppermute | solution.py:23
  (63 other events, 387.8 us)
Sparse Core Ops, SparseCore 0:
  10.6 164.0 all-reduce.8
  401.3 300.7 all-reduce.10
where the time goes:
time: 727 us; the launch traced here: 716 us
  waiting for transfers between devices  483 us (66%)
  other arithmetic  82 us (11%)
  local copies, waits for them, and re-layouts  59.2 us (8%)
  matrix products  40.1 us (6%)
  starting transfers between devices  36.1 us (5%)
  between operations  15.9 us (2%)
    unnamed x3, waiting for transfers between devices  301 us
    psum x1, waiting for transfers between devices, broadcast(): return lax.psum(jnp.where(mine, x, jnp.zeros_like(x)), axis)  159 us
    scatter-add x8, other arithmetic, per_device(): grad_messages.at[enc_source[:, arc_location]]  39.7 us
    gather x8, local copies, waits for them, and re-layouts, per_device(): messages[enc_source[:, arc_location]].astype(jnp.float32)  24.1 us
    scatter-add x3, other arithmetic, per_device(): grad_dnorm_ext.at[unpacker_start_cell[:, arc_location]]  15.8 us
    ppermute x5, starting transfers between devices, extended(): lax.ppermute(lax.slice_in_dim(block, block.shape[dim] - width, None, axis...  15.6 us
  transfers between devices with their start and end apart: 14, of which 10 were waited for; matrix products, arithmetic and copies ran while one was open for 2% of the time, Pallas kernels for 0%

commit v1 on v0

--- a/solution.py
+++ b/solution.py
@@ -2,6 +2,7 @@
 import jax.numpy as jnp
 from jax import lax
 from jax.sharding import PartitionSpec as P
+from jax.lax import all_gather
 
 HEAD_DIM = 64
 RIM_G = 128
@@ -27,7 +28,11 @@
 
 def broadcast(x, axis, root):
     mine = lax.axis_index(axis) == root
-    return lax.psum(jnp.where(mine, x, jnp.zeros_like(x)), axis)
+
+    def terms_expand(field_in):
+        return all_gather(field_in, axis_name=axis).sum(axis=0)
+
+    return terms_expand(jnp.where(mine, x, jnp.zeros_like(x)))
 
 
 def rms_factor(values):

time: 727 us -> 649 us (0.89)
  waiting for transfers between devices: 483 us -> 404 us
    psum x1 -> x0, waiting for transfers between devices: 159 us -> none  [broadcast(): return lax.psum(jnp.where(mine, x, jnp.zeros_like(x)), axis)]
    all_gather x0 -> x1, waiting for transfers between devices: none -> 78.9 us  [terms_expand(): return all_gather(field_in, axis_name=axis).sum(axis=0)]
where the time goes in v1:
time: 649 us; the launch traced here: 638 us
  waiting for transfers between devices  404 us (62%)
  other arithmetic  83.9 us (13%)
  local copies, waits for them, and re-layouts  57.9 us (9%)
  matrix products  40.1 us (6%)
  starting transfers between devices  36.2 us (6%)
  between operations  15.9 us (2%)
    unnamed x3, waiting for transfers between devices  301 us
    all_gather x1, waiting for transfers between devices, terms_expand(): return all_gather(field_in, axis_name=axis).sum(axis=0)  78.9 us
    scatter-add x8, other arithmetic, per_device(): grad_messages.at[enc_source[:, arc_location]]  39.7 us
    gather x8, local copies, waits for them, and re-layouts, per_device(): messages[enc_source[:, arc_location]].astype(jnp.float32)  24.1 us
    ppermute x5, starting transfers between devices, extended(): lax.ppermute(lax.slice_in_dim(block, block.shape[dim] - width, None, axis...  15.9 us
    scatter-add x3, other arithmetic, per_device(): grad_dnorm_ext.at[unpacker_start_cell[:, arc_location]]  15.8 us
    all_to_all x2, waiting for transfers between devices, realization_rotate(): lax.all_to_all(values.astype(jnp.bfloat16), 'member', split_axis=0, conca...  13.9 us
  transfers between devices with their start and end apart: 14, of which 10 were waited for; matrix products, arithmetic and copies ran while one was open for 2% of the time, Pallas kernels for 0%

profile of v1, /device:TPU:8, one launch (start us, length us, event | category | flops | bytes accessed | tf_op | source)
XLA Modules:
  0.0 637.7 jit_solution(4973830997766377873)
XLA Ops:
  16.5 78.9 %all-gather.2.cloned.1.call-done = bf16[16,256,256]{2,1,0:T(8,128)(2,1)} async-done(((bf16[1,256,256]{2,1,0:T(8,128)(2,1)}), bf16[16,256,256]{2,1,0:T(8,128)(2,1)}) %all-gather.2.cloned.1.call-update) | async-done | bytes 2097168 | tf_op jit(solution)/shard_map/all_gather | solution.py:33
  136.9 3.8 collective-permute-done.2
  154.4 3.6 gather_fusion.8
  167.8 6.5 %all-to-all-start = ((bf16[16,16,128]{2,1,0:T(8,128)(2,1)}), bf16[16,16,128]{2,1,0:T(8,128)(2,1)}, u32[]{:S(2)}, u32[]{:S(2)}) async-start(bf16[16,16,128]{2,1,0:T(8,128)(2,1)} %bitcast.157), calls=%async_computation | async-start | bytes 131072 | tf_op jit(solution)/shard_map/all_to_all | solution.py:73
  175.1 7.8 %all-to-all-done = bf16[16,16,128]{2,1,0:T(8,128)(2,1)} async-done(((bf16[16,16,128]{2,1,0:T(8,128)(2,1)}), bf16[16,16,128]{2,1,0:T(8,128)(2,1)}, u32[]{:S(2)}, u32[]{:S(2)}) %all-to-all-start) | async-done | bytes 65568 | tf_op jit(solution)/shard_map/all_to_all | solution.py:73
  185.6 4.1 all-to-all-start.1
  192.1 6.1 all-to-all-done.1
  200.5 4.6 scatter_custom_fusion
  205.1 5.6 scatter_custom_fusion.1
  210.7 5.6 scatter_custom_fusion.2
  217.7 5.7 collective-permute-start.6
  238.9 6.6 %collective-permute-start.8 = (bf16[64,1024]{0,1:T(8,128)(2,1)S(1)}, bf16[64,1024]{0,1:T(8,128)(2,1)S(1)}, u32[]{:S(2)}, u32[]{:S(2)}) collective-permute-start(bf16[64,1024]{0,1:T(8,128)(2,1)S(1)} %get-tuple-element.107), channel_id=1, source_target_pairs={{0,1},{1,2},{2,3},{3,4},{4,5},{5,6},{6,7},{7,8},{8,9},{9,10},{10,1... | collective-permute-start | bytes 393224 | tf_op jit(solution)/shard_map/ppermute | solution.py:21
  245.5 6.0 collective-permute-start.9
  271.0 3.7 fusion.87
  278.0 3.7 scatter_custom_fusion.3
  281.7 5.1 scatter_custom_fusion.4
  286.8 5.1 scatter_custom_fusion.5
  291.9 5.1 scatter_custom_fusion.6
  297.0 5.1 scatter_custom_fusion.7
  302.2 5.1 scatter_custom_fusion.8
  307.3 5.3 scatter_custom_fusion.9
  312.6 5.1 scatter_custom_fusion.10
  317.8 5.2 fusion.3
  323.0 301.0 %all-reduce.8.cloned.1.call-done = (f32[16,1024]{1,0:T(8,128)}, f32[128,1024]{0,1:T(8,128)}, f32[1024,1536]{1,0:T(8,128)}, f32[512,1024]{0,1:T(8,128)}, f32[1024,128]{1,0:T(8,128)}) async-done(((f32[16,1024]{1,0:T(8,128)}, f32[128,1024]{0,1:T(8,128)}, f32[1024,1536]{1,0:T(8,128)}, f32[512,1024]{0,1:T(8,128)}, f32[1024,128]{1,0:T(8,128)}), (f32[16,1024]{1,0:T(8,128)}, f32[128,1024]{0,1:T(8,128)}, ...) | async-done | bytes 9502736
  (274 shorter events, 127.2 us)
Async XLA Ops:
  7.2 124.7 %copy-start = (bf16[1024,1536]{1,0:T(8,128)(2,1)S(1)}, bf16[1024,1536]{1,0:T(8,128)(2,1)}, u32[]{:S(2)}) copy-start(bf16[1024,1536]{1,0:T(8,128)(2,1)} %param.32) | copy-start | bytes 9437188
  7.2 88.3 %all-gather.2.cloned.1.call-start = ((), (), s32[]{:S(2)}) async-start(), calls=%async_computation.2 | async-start | bytes 2228224 | tf_op jit(solution)/shard_map/all_gather | solution.py:33
  11.4 92.7 %copy-start.59 = (s32[128]{0:T(128)}, s32[128]{0:T(128)S(1)}, u32[]{:S(2)}) copy-start(s32[128]{0:T(128)S(1)} %get-tuple-element.141) | copy-start | bytes 1540
  15.0 113.3 %copy-start.32 = (f32[128]{0:T(128)}, f32[128]{0:T(128)S(1)}, u32[]{:S(2)}) copy-start(f32[128]{0:T(128)S(1)} %get-tuple-element.132) | copy-start | bytes 1540
  15.0 113.3 %copy-start.34 = (f32[128]{0:T(128)}, f32[128]{0:T(128)S(1)}, u32[]{:S(2)}) copy-start(f32[128]{0:T(128)S(1)} %get-tuple-element.138) | copy-start | bytes 1540
  15.0 113.3 %copy-start.36 = (f32[128]{0:T(128)}, f32[128]{0:T(128)S(1)}, u32[]{:S(2)}) copy-start(f32[128]{0:T(128)S(1)} %get-tuple-element.139) | copy-start | bytes 1540
  15.0 113.2 %copy-start.38 = (f32[128]{0:T(128)}, f32[128]{0:T(128)S(1)}, u32[]{:S(2)}) copy-start(f32[128]{0:T(128)S(1)} %get-tuple-element.133) | copy-start | bytes 1540
  15.1 113.2 %copy-start.40 = (f32[128]{0:T(128)}, f32[128]{0:T(128)S(1)}, u32[]{:S(2)}) copy-start(f32[128]{0:T(128)S(1)} %get-tuple-element.134) | copy-start | bytes 1540
  15.1 113.2 %copy-start.42 = (f32[128]{0:T(128)}, f32[128]{0:T(128)S(1)}, u32[]{:S(2)}) copy-start(f32[128]{0:T(128)S(1)} %get-tuple-element.135) | copy-start | bytes 1540
  15.1 113.2 %copy-start.44 = (f32[128]{0:T(128)}, f32[128]{0:T(128)S(1)}, u32[]{:S(2)}) copy-start(f32[128]{0:T(128)S(1)} %get-tuple-element.136) | copy-start | bytes 1540
  15.1 113.2 %copy-start.46 = (f32[128]{0:T(128)}, f32[128]{0:T(128)S(1)}, u32[]{:S(2)}) copy-start(f32[128]{0:T(128)S(1)} %get-tuple-element.137) | copy-start | bytes 1540
  97.4 3.4 collective-permute-start
  97.4 3.3 collective-permute-start.1
  134.8 5.9 collective-permute-start.2
  136.4 4.3 collective-permute-start.3
  148.6 4.9 collective-permute-start.4
  150.4 3.1 collective-permute-start.5
  167.8 15.0 %all-to-all-start = ((bf16[16,16,128]{2,1,0:T(8,128)(2,1)}), bf16[16,16,128]{2,1,0:T(8,128)(2,1)}, u32[]{:S(2)}, u32[]{:S(2)}) async-start(bf16[16,16,128]{2,1,0:T(8,128)(2,1)} %bitcast.157), calls=%async_computation | async-start | bytes 131072 | tf_op jit(solution)/shard_map/all_to_all | solution.py:73
  185.6 12.6 %all-to-all-start.1 = ((bf16[16,16,128]{2,1,0:T(8,128)(2,1)}), bf16[16,16,128]{2,1,0:T(8,128)(2,1)}, u32[]{:S(2)}, u32[]{:S(2)}) async-start(bf16[16,16,128]{2,1,0:T(8,128)(2,1)} %multiply_convert_fusion.4), calls=%async_computation.1 | async-start | bytes 131072 | tf_op jit(solution)/shard_map/all_to_all | solution.py:73
  189.8 434.2 %all-reduce.8.cloned.1.call-start = ((), (), s32[]{:S(2)}) async-start(), calls=%async_computation.3 | async-start | bytes 19005440
  217.7 9.6 %collective-permute-start.6 = (bf16[64,1024]{1,0:T(8,128)(2,1)S(1)}, bf16[64,1024]{1,0:T(8,128)(2,1)S(1)}, u32[]{:S(2)}, u32[]{:S(2)}) collective-permute-start(bf16[64,1024]{1,0:T(8,128)(2,1)S(1)} %get-tuple-element.109), channel_id=1, source_target_pairs={{0,1},{1,2},{2,3},{3,4},{4,5},{5,6},{6,7},{7,8},{8,9},{9,10},{10,1... | collective-permute-start | bytes 393224 | tf_op jit(solution)/shard_map/ppermute | solution.py:21
  223.4 3.9 collective-permute-start.7
  238.9 16.2 %collective-permute-start.8 = (bf16[64,1024]{0,1:T(8,128)(2,1)S(1)}, bf16[64,1024]{0,1:T(8,128)(2,1)S(1)}, u32[]{:S(2)}, u32[]{:S(2)}) collective-permute-start(bf16[64,1024]{0,1:T(8,128)(2,1)S(1)} %get-tuple-element.107), channel_id=1, source_target_pairs={{0,1},{1,2},{2,3},{3,4},{4,5},{5,6},{6,7},{7,8},{8,9},{9,10},{10,1... | collective-permute-start | bytes 393224 | tf_op jit(solution)/shard_map/ppermute | solution.py:21
  245.5 9.9 %collective-permute-start.9 = (bf16[64,1024]{0,1:T(8,128)(2,1)S(1)}, bf16[64,1024]{0,1:T(8,128)(2,1)S(1)}, u32[]{:S(2)}, u32[]{:S(2)}) collective-permute-start(bf16[64,1024]{0,1:T(8,128)(2,1)S(1)} %get-tuple-element.108), channel_id=1, source_target_pairs={{1,0},{2,1},{3,2},{4,3},{5,4},{6,5},{7,6},{8,7},{9,8},{10,9},{11,1... | collective-permute-start | bytes 393224 | tf_op jit(solution)/shard_map/ppermute | solution.py:24
  (64 other events, 361.0 us)
Sparse Core Ops, SparseCore 0:
  9.8 85.6 all-gather.1
  323.1 300.8 all-reduce.7
